TPU v7x, 32 devices: a whole 2x2x4 slice. The times are simulated.
32 devices in a mesh: groups: 2 (over y), seq: 4 (over z), dp: 2 (over x), fsdp: 2 (over core).
Axes of the slice: x: 2, y: 2, z: 4, core: 2. Of those that a mesh axis runs over, the one named last changes fastest.
Arguments:
- tokens: bfloat16 [8, 4, 8, 16, 1024], P(('groups', 'dp', 'fsdp'), 'seq'), parts along dimension 0, may hold values from -6 to 6
- timesteps: int32 [8], P(('groups', 'dp', 'fsdp')), parts along dimension 0, may hold values from 0 to 999
- pxrd_mod: float32 [8, 3, 1024], P(('groups', 'dp', 'fsdp')), parts along dimension 0, may hold values from -3 to 3
- time_weight: bfloat16 [256, 3072], P('fsdp'), may hold values from -0.375 to 0.375
- conv_kernel: float32 [27, 1024], replicated, may hold values from -0.9 to 0.9
- qkv_weight: bfloat16 [1024, 1536], P('fsdp'), may hold values from -0.75 to 0.75
- out_weight: bfloat16 [512, 1024], P('fsdp'), may hold values from -1 to 1
- out_cot: bfloat16 [8, 4, 8, 16, 1024], P(('groups', 'dp', 'fsdp'), 'seq'), parts along dimension 0, may hold values from -6 to 6
Outputs:
- out_tokens: bfloat16 [8, 4, 8, 16, 1024], P(('groups', 'dp', 'fsdp'), 'seq'), parts along dimension 0
- d_tokens: bfloat16 [8, 4, 8, 16, 1024], P(('groups', 'dp', 'fsdp'), 'seq'), parts along dimension 0
- d_kernel: float32 [54, 1024], P('groups'), parts along dimension 0
There are 2 independent parts, one for each index of `groups`. A program takes and returns all parts, laid end to end along the dimension named above; an argument that names none is the same for every part. Nothing has to cross between parts.
All inputs are finite; a program needn't handle non-finite values.
Results may differ from a plain program's by a relative error of at most 0.024.
Values may be sent and summed in bfloat16 or wider, within the bound.
No kernel may reach another device: no remote copies, remote signals or barrier semaphores. Data moves between devices by JAX's collectives and lax.ppermute only.
A program may use at most 64 MiB of HBM per device.

v0:
```python
import math
import jax
import jax.numpy as jnp
from jax import lax
from jax.sharding import PartitionSpec as P

H = 8
HD = 64


def padded_2(value, sides, width):
    for axis, dim in sides:
        count, length = (lax.axis_size(axis), value.shape[dim])
        up = [(i, (i + 1) % count) for i in range(count - 1)]
        down = [(j, i) for i, j in up]
        last = lax.slice_in_dim(value, length - width, length, axis=dim)
        leading = lax.slice_in_dim(value, 0, width, axis=dim)
        before = lax.ppermute(last, axis, up)
        after = lax.ppermute(leading, axis, down)
        value = jnp.concatenate([before, value, after], axis=dim)
    return value


def time_features(steps_int, freq_width):
    half_width = freq_width // 2
    freq_index = jnp.arange(half_width).astype(jnp.float32)
    frequency = jnp.exp(freq_index * (-math.log(10000.0) / half_width))
    angles = steps_int.astype(jnp.float32)[:, None] * frequency[None, :]
    return jnp.concatenate([jnp.cos(angles), jnp.sin(angles)], axis=1).astype(jnp.bfloat16)


def modulation(steps_int, pxrd_mod, time_weight):
    features = time_features(steps_int, time_weight.shape[0])
    projected = jnp.dot(features, time_weight, preferred_element_type=jnp.float32)
    return projected.reshape(steps_int.shape[0], 3, time_weight.shape[1] // 3) + pxrd_mod


def depthwise(padded_z, kernel_taps, plane_count):
    framed = jnp.pad(padded_z, ((0, 0), (1, 1), (1, 1), (0, 0)))
    side_y = framed.shape[1] - 2
    side_x = framed.shape[2] - 2
    result = jnp.zeros((plane_count, side_y, side_x, framed.shape[3]), jnp.float32)
    for tap_z in range(3):
        for tap_y in range(3):
            for tap_x in range(3):
                window = framed[
                    tap_z : tap_z + plane_count, tap_y : tap_y + side_y, tap_x : tap_x + side_x
                ]
                result = result + kernel_taps[9 * tap_z + 3 * tap_y + tap_x] * window.astype(
                    jnp.float32
                )
    return result


def kernel_terms(padded_z, upstream, plane_count):
    framed = jnp.pad(padded_z, ((0, 0), (1, 1), (1, 1), (0, 0)))
    side_y = framed.shape[1] - 2
    side_x = framed.shape[2] - 2
    upstream_f = upstream.astype(jnp.float32)
    collected = []
    for tap_z in range(3):
        for tap_y in range(3):
            for tap_x in range(3):
                window = framed[
                    tap_z : tap_z + plane_count, tap_y : tap_y + side_y, tap_x : tap_x + side_x
                ]
                collected.append(jnp.sum(window.astype(jnp.float32) * upstream_f, axis=(0, 1, 2)))
    return jnp.stack(collected)


def modulate(stream, shift_row, scale_row):
    centre = stream - jnp.mean(stream, axis=-1, keepdims=True)
    spread = jnp.mean(centre * centre, axis=-1, keepdims=True)
    return centre * lax.rsqrt(spread + 1e-06) * (1.0 + scale_row) + shift_row


def head_norms(projected):
    row_count = projected.shape[0]
    sections = projected.reshape(row_count, 3, H, HD)
    query_key = sections[:, :2]
    normed = query_key * lax.rsqrt(jnp.mean(query_key * query_key, axis=-1, keepdims=True) + 1e-06)
    return (
        normed[:, 0].reshape(row_count, H * HD),
        normed[:, 1].reshape(row_count, H * HD),
        sections[:, 2].reshape(row_count, H * HD),
    )


def attend_both(queries, grads, key_rows, value_rows):
    count = queries.shape[0]
    heads = queries.shape[1]
    block = min(512, count)
    steps = count // block
    scale_dot = 1.0 / math.sqrt(HD)

    def one_block(carry, pieces):
        query_blk, grad_blk = pieces
        scores = (
            jnp.einsum("qhd,khd->hqk", query_blk, key_rows, preferred_element_type=jnp.float32)
            * scale_dot
        )
        expo = jnp.exp(scores)
        totals = jnp.sum(expo, axis=-1, keepdims=True)
        weights = expo / totals
        probs = weights.astype(jnp.bfloat16)
        attn_blk = jnp.einsum(
            "hqk,khd->qhd", probs, value_rows, preferred_element_type=jnp.float32
        ).astype(jnp.bfloat16)
        delta = jnp.sum(grad_blk.astype(jnp.float32) * attn_blk.astype(jnp.float32), axis=-1).T
        dprob = jnp.einsum("qhd,khd->hqk", grad_blk, value_rows, preferred_element_type=jnp.float32)
        dscore = (weights * (dprob - delta[:, :, None]) * scale_dot).astype(jnp.bfloat16)
        dquery = jnp.einsum("hqk,khd->qhd", dscore, key_rows, preferred_element_type=jnp.float32)
        dkey = carry[0] + jnp.einsum(
            "hqk,qhd->khd", dscore, query_blk, preferred_element_type=jnp.float32
        )
        dvalue = carry[1] + jnp.einsum(
            "hqk,qhd->khd", probs, grad_blk, preferred_element_type=jnp.float32
        )
        return ((dkey, dvalue), (attn_blk, dquery))

    zeros_kv = jnp.zeros(key_rows.shape, jnp.float32)
    (dkey, dvalue), (attn_all, dquery) = lax.scan(
        one_block,
        (zeros_kv, zeros_kv),
        (queries.reshape(steps, block, heads, HD), grads.reshape(steps, block, heads, HD)),
    )
    return (attn_all.reshape(count, heads, HD), dquery.reshape(count, heads, HD), dkey, dvalue)


def shards(tokens, timesteps, pxrd_mod, time_weight, conv_kernel, qkv_weight, out_weight, out_cot):
    w_qkv, w_out, w_time = (
        lax.all_gather(qkv_weight, "fsdp", axis=0, tiled=True),
        lax.all_gather(out_weight, "fsdp", axis=0, tiled=True),
        lax.all_gather(time_weight, "fsdp", axis=0, tiled=True),
    )
    plane_count = tokens.shape[1]
    side_y = tokens.shape[2]
    side_x = tokens.shape[3]
    width_model = tokens.shape[4]
    row_count = plane_count * side_y * side_x
    inner_width = H * HD
    seq_count = lax.axis_size("seq")
    head_groups = min(H, seq_count)
    per_device = H // head_groups
    row_split = seq_count // head_groups
    part_rows = row_count // row_split
    group_width = per_device * HD
    padded = padded_2(tokens, (("seq", 1),), 1)[0]
    mixed = depthwise(padded, conv_kernel, plane_count)
    resid = (
        (tokens[0].astype(jnp.float32) + mixed).astype(jnp.bfloat16).reshape(row_count, width_model)
    )
    modul = modulation(timesteps, pxrd_mod, w_time)
    shift_row = modul[0, 0]
    scale_row = modul[0, 1]
    gate_row = modul[0, 2]
    resid_f = resid.astype(jnp.float32)
    normed = modulate(resid_f, shift_row, scale_row).astype(jnp.bfloat16)
    projected = jnp.dot(normed, w_qkv, preferred_element_type=jnp.float32)
    query_f, key_f, value_f = head_norms(projected)
    cotangent = out_cot[0].reshape(row_count, width_model).astype(jnp.float32)
    gated = (gate_row * cotangent).astype(jnp.bfloat16)
    grad_attn = lax.dot_general(
        gated, w_out, (((1,), (1,)), ((), ())), preferred_element_type=jnp.float32
    ).astype(jnp.bfloat16)

    def to_heads(token_rows):
        shaped = token_rows.reshape(row_split, part_rows, head_groups, group_width)
        return shaped.transpose(2, 0, 1, 3).reshape(seq_count, part_rows, group_width)

    def from_heads(head_rows):
        shaped = head_rows.reshape(head_groups, row_split, part_rows, group_width)
        return shaped.transpose(1, 2, 0, 3).reshape(row_count, inner_width)

    query_heads, grad_heads = (
        lax.all_to_all(
            to_heads(query_f.astype(jnp.bfloat16)), "seq", split_axis=0, concat_axis=0, tiled=True
        ),
        lax.all_to_all(to_heads(grad_attn), "seq", split_axis=0, concat_axis=0, tiled=True),
    )
    query_count = seq_count * part_rows
    query_heads = query_heads.reshape(query_count, per_device, HD)
    grad_heads = grad_heads.reshape(query_count, per_device, HD)
    stacked = jnp.stack(
        [
            key_f.astype(jnp.bfloat16).reshape(row_count, head_groups, group_width),
            value_f.astype(jnp.bfloat16).reshape(row_count, head_groups, group_width),
        ],
        axis=2,
    )
    by_group = stacked.transpose(1, 0, 2, 3).reshape(head_groups, row_count, 2 * group_width)
    copies = jnp.broadcast_to(
        by_group[:, None], (head_groups, row_split, row_count, 2 * group_width)
    )
    arrived = lax.all_to_all(
        copies.reshape(seq_count, row_count, 2 * group_width),
        "seq",
        split_axis=0,
        concat_axis=0,
        tiled=True,
    )
    key_value = arrived.reshape(seq_count * row_count, 2, per_device, HD)
    attn_heads, dquery, dkey, dvalue = attend_both(
        query_heads, grad_heads, key_value[:, 0], key_value[:, 1]
    )
    attn_tok = from_heads(
        lax.all_to_all(
            attn_heads.reshape(seq_count, part_rows, group_width),
            "seq",
            split_axis=0,
            concat_axis=0,
            tiled=True,
        )
    )
    projected_out = jnp.dot(attn_tok, w_out, preferred_element_type=jnp.float32)
    out_rows = (resid_f + gate_row * projected_out).astype(jnp.bfloat16)
    dquery_tok = from_heads(
        lax.all_to_all(
            dquery.reshape(seq_count, part_rows, group_width),
            "seq",
            split_axis=0,
            concat_axis=0,
            tiled=True,
        )
    )
    grads_kv = jnp.stack([dkey, dvalue], axis=1)
    returned = lax.all_to_all(
        grads_kv.reshape(seq_count, row_count, 2 * group_width).astype(jnp.bfloat16),
        "seq",
        split_axis=0,
        concat_axis=0,
        tiled=True,
    ).astype(jnp.float32)
    summed = jnp.sum(returned.reshape(head_groups, row_split, row_count, 2 * group_width), axis=1)
    grads_tok = (
        summed.reshape(head_groups, row_count, 2, group_width)
        .transpose(2, 1, 0, 3)
        .reshape(2, row_count, inner_width)
    )
    _, pullback = jax.vjp(head_norms, projected)
    (grad_projected,) = pullback((dquery_tok, grads_tok[0], grads_tok[1]))
    grad_proj_b = grad_projected.astype(jnp.bfloat16)
    grad_normed = lax.dot_general(
        grad_proj_b, w_qkv, (((1,), (1,)), ((), ())), preferred_element_type=jnp.float32
    )
    _, pull_norm = jax.vjp(lambda stream: modulate(stream, shift_row, scale_row), resid_f)
    (grad_stream,) = pull_norm(grad_normed)
    grad_resid = (
        (cotangent + grad_stream)
        .astype(jnp.bfloat16)
        .reshape(1, plane_count, side_y, side_x, width_model)
    )
    grad_padded = padded_2(grad_resid, (("seq", 1),), 1)[0]
    grad_tokens = (
        grad_resid[0].astype(jnp.float32) + depthwise(grad_padded, conv_kernel[::-1], plane_count)
    ).astype(jnp.bfloat16)
    local_terms = kernel_terms(padded, grad_resid[0], plane_count)
    norm_factor = 1.0 / math.sqrt(
        lax.axis_size("dp") * lax.axis_size("fsdp") * seq_count * row_count
    )
    grad_kernel = lax.psum(local_terms, ("seq", "dp", "fsdp")) * norm_factor
    return (out_rows.reshape(tokens.shape), grad_tokens.reshape(tokens.shape), grad_kernel)


def solution(mesh):
    placed = (
        P(("groups", "dp", "fsdp"), "seq", None, None, None),
        P(("groups", "dp", "fsdp")),
        P(("groups", "dp", "fsdp"), None, None),
        P("fsdp", None),
        P(),
        P("fsdp", None),
        P("fsdp", None),
        P(("groups", "dp", "fsdp"), "seq", None, None, None),
    )
    return jax.shard_map(
        shards,
        mesh=mesh,
        in_specs=placed,
        out_specs=(
            P(("groups", "dp", "fsdp"), "seq", None, None, None),
            P(("groups", "dp", "fsdp"), "seq", None, None, None),
            P("groups", None),
        ),
        check_vma=False,
    )
```

profile of v0, /device:TPU:8, one launch (start us, length us, event | category | flops | bytes accessed | tf_op | source)
XLA Modules:
  0.0 221.3 jit_solution(6687539041669319922)
XLA Ops:
  7.2 2.3 %copy.35 = bf16[128,3072]{0,1:T(8,128)(2,1)} copy(bf16[128,3072]{1,0:T(8,128)(2,1)} %param.11) | data formatting | bytes 1572864 | tf_op args[3]
  9.6 0.7 all-gather.8.cloned.1.call-update
  10.3 0.7 all-gather.6.cloned.1.call-update
  11.0 3.5 %collective-permute-start = (bf16[1,1,8,16,1024]{4,3,2,1,0:T(8,128)(2,1)S(1)}, bf16[1,1,8,16,1024]{4,3,2,1,0:T(8,128)(2,1)S(1)}, u32[]{:S(2)}, u32[]{:S(2)}) collective-permute-start(bf16[1,1,8,16,1024]{4,3,2,1,0:T(8,128)(2,1)S(1)} %copy-done.6), channel_id=1, source_target_pairs={{0,4},{4,8},{8,12},{1,5},{5,9},{9,13},{2,6},{6,10},{10,14},{3,7},{... | collective-permute-start | bytes 786440 | tf_op jit(solution)/shard_map/ppermute | solution.py:18
  14.5 2.4 %collective-permute-start.1 = (bf16[1,1,8,16,1024]{4,3,2,1,0:T(8,128)(2,1)S(1)}, bf16[1,1,8,16,1024]{4,3,2,1,0:T(8,128)(2,1)S(1)}, u32[]{:S(2)}, u32[]{:S(2)}) collective-permute-start(bf16[1,1,8,16,1024]{4,3,2,1,0:T(8,128)(2,1)S(1)} %copy-done.6), channel_id=1, source_target_pairs={{4,0},{8,4},{12,8},{5,1},{9,5},{13,9},{6,2},{10,6},{14,10},{7,3},{... | collective-permute-start | bytes 786440 | tf_op jit(solution)/shard_map/ppermute | solution.py:19
  18.0 3.0 %collective-permute-done = bf16[1,1,8,16,1024]{4,3,2,1,0:T(8,128)(2,1)S(1)} collective-permute-done((bf16[1,1,8,16,1024]{4,3,2,1,0:T(8,128)(2,1)S(1)}, bf16[1,1,8,16,1024]{4,3,2,1,0:T(8,128)(2,1)S(1)}, u32[]{:S(2)}, u32[]{:S(2)}) %collective-permute-start) | collective-permute-done | bytes 262176 | tf_op jit(solution)/shard_map/ppermute | solution.py:18
  21.0 3.2 %collective-permute-done.1 = bf16[1,1,8,16,1024]{4,3,2,1,0:T(8,128)(2,1)S(1)} collective-permute-done((bf16[1,1,8,16,1024]{4,3,2,1,0:T(8,128)(2,1)S(1)}, bf16[1,1,8,16,1024]{4,3,2,1,0:T(8,128)(2,1)S(1)}, u32[]{:S(2)}, u32[]{:S(2)}) %collective-permute-start.1) | collective-permute-done | bytes 262176 | tf_op jit(solution)/shard_map/ppermute | solution.py:19
  24.2 0.1 maximum_bitcast_fusion
  24.3 0.9 copy-done.1
  25.2 2.7 %convert_reduce_fusion = (f32[8,16]{1,0:T(8,128)S(1)}, bf16[1,8,16,1024]{3,2,1,0:T(8,128)(2,1)S(1)}) fusion(f32[1024]{0:T(1024)S(1)} %bitcast.275, f32[1024]{0:T(1024)S(1)} %bitcast.277, f32[1024]{0:T(1024)S(1)} %bitcast.281, f32[1024]{0:T(1024)S(1)} %bitcast.283, bf16[1,1,8,16,1024]{4,3,2,1,0:T(8,128)(2,1)S(1)} %collective-permute-done.1, ...), kind=kLoop, calls=%fused_computation.221 | loop fusion | flops 11009920 | bytes 1946112 | tf_op jit(solution)/shard_map/reduce_sum | solution.py:72
  28.2 0.2 multiply_reduce_fusion.3
  28.4 0.6 multiply_add_fusion.1
  29.0 2.0 fusion.103
  31.1 1.5 all-gather.8.cloned.1.call-done
  32.6 1.7 convolution_convert_fusion.2
  34.3 0.8 copy.58
  35.1 5.2 %all-to-all-start.3 = ((bf16[4,128,128]{1,2,0:T(8,128)(2,1)}), bf16[4,128,128]{1,2,0:T(8,128)(2,1)S(1)}, u32[]{:S(2)}, u32[]{:S(2)}) async-start(bf16[4,128,128]{1,2,0:T(8,128)(2,1)} %bitcast.65), calls=%async_computation.3 | async-start | bytes 262144 | tf_op jit(solution)/shard_map/all_to_all | solution.py:179
  40.2 0.9 add_convert_fusion.1
  41.2 6.3 %all-gather.6.cloned.1.call-done = bf16[1024,1536]{1,0:T(8,128)(2,1)} async-done(((bf16[512,1536]{1,0:T(8,128)(2,1)}), bf16[1024,1536]{1,0:T(8,128)(2,1)}) %all-gather.6.cloned.1.call-update) | async-done | bytes 3145744 | tf_op jit(solution)/shard_map/all_gather | solution.py:132
  47.5 3.2 %copy.36 = bf16[1536,1024]{1,0:T(8,128)(2,1)S(1)} copy(bf16[1536,1024]{0,1:T(8,128)(2,1)} %bitcast.242) | data formatting | bytes 6291456 | tf_op jit(solution)/shard_map/dot_general | solution.py:159
  50.7 1.9 fusion.104
  52.7 0.8 copy-done.3
  53.6 0.7 fusion.98
  54.2 5.1 %all-to-all-start.1 = ((bf16[4,128,128]{1,2,0:T(8,128)(2,1)}), bf16[4,128,128]{1,2,0:T(8,128)(2,1)S(1)}, u32[]{:S(2)}, u32[]{:S(2)}) async-start(bf16[4,128,128]{1,2,0:T(8,128)(2,1)} %bitcast.54), calls=%async_computation.1 | async-start | bytes 262144 | tf_op jit(solution)/shard_map/all_to_all | solution.py:176
  59.4 1.0 slice.712
  60.3 0.7 pad_maximum_fusion
  61.1 3.6 %all-to-all-done.1 = bf16[4,128,128]{1,2,0:T(8,128)(2,1)S(1)} async-done(((bf16[4,128,128]{1,2,0:T(8,128)(2,1)}), bf16[4,128,128]{1,2,0:T(8,128)(2,1)S(1)}, u32[]{:S(2)}, u32[]{:S(2)}) %all-to-all-start.1) | async-done | bytes 131104 | tf_op jit(solution)/shard_map/all_to_all | solution.py:176
  64.6 4.5 %all-to-all-start = ((bf16[4,128,256]{1,2,0:T(8,128)(2,1)}), bf16[4,128,256]{1,2,0:T(8,128)(2,1)S(1)}, u32[]{:S(2)}, u32[]{:S(2)}) async-start(bf16[4,128,256]{1,2,0:T(8,128)(2,1)} %bitcast.50), calls=%async_computation | async-start | bytes 524288 | tf_op jit(solution)/shard_map/all_to_all | solution.py:195
  69.1 0.1 copy.44
  69.3 0.1 copy.40
  69.5 6.0 %all-to-all-done = bf16[4,128,256]{1,2,0:T(8,128)(2,1)S(1)} async-done(((bf16[4,128,256]{1,2,0:T(8,128)(2,1)}), bf16[4,128,256]{1,2,0:T(8,128)(2,1)S(1)}, u32[]{:S(2)}, u32[]{:S(2)}) %all-to-all-start) | async-done | bytes 262176 | tf_op jit(solution)/shard_map/all_to_all | solution.py:195
  75.4 0.2 copy.39
  75.7 0.1 reshape.516
  75.8 0.5 fusion.1
  76.3 0.3 fusion.7
  76.6 0.4 fusion.6
  77.1 0.3 multiply_reduce_fusion.4
  77.4 0.7 multiply_convert_fusion
  78.1 0.4 fusion.5
  78.6 0.7 copy.48
  79.4 5.2 %all-to-all-start.4 = ((bf16[4,128,256]{1,2,0:T(8,128)(2,1)}), bf16[4,128,256]{1,2,0:T(8,128)(2,1)S(1)}, u32[]{:S(2)}, u32[]{:S(2)}) async-start(bf16[4,128,256]{1,2,0:T(8,128)(2,1)} %copy.48), calls=%async_computation.4 | async-start | bytes 524288 | tf_op jit(solution)/shard_map/all_to_all | solution.py:227
  84.6 0.1 div.54
  84.8 0.3 convolution_bitcast_fusion
  85.1 0.1 reshape_reshape.12
  85.2 0.7 copy.50
  85.9 0.7 copy.42
  86.6 4.2 %all-to-all-done.4 = bf16[4,128,256]{1,2,0:T(8,128)(2,1)S(1)} async-done(((bf16[4,128,256]{1,2,0:T(8,128)(2,1)}), bf16[4,128,256]{1,2,0:T(8,128)(2,1)S(1)}, u32[]{:S(2)}, u32[]{:S(2)}) %all-to-all-start.4) | async-done | bytes 262176 | tf_op jit(solution)/shard_map/all_to_all | solution.py:227
  90.8 4.0 %all-to-all-start.5 = ((f32[4,128,128]{1,2,0:T(8,128)}), f32[4,128,128]{1,2,0:T(8,128)S(1)}, u32[]{:S(2)}, u32[]{:S(2)}) async-start(f32[4,128,128]{1,2,0:T(8,128)} %copy.50), calls=%async_computation.5 | async-start | bytes 524288 | tf_op jit(solution)/shard_map/all_to_all | solution.py:218
  94.9 6.1 %all-to-all-done.5 = f32[4,128,128]{1,2,0:T(8,128)S(1)} async-done(((f32[4,128,128]{1,2,0:T(8,128)}), f32[4,128,128]{1,2,0:T(8,128)S(1)}, u32[]{:S(2)}, u32[]{:S(2)}) %all-to-all-start.5) | async-done | bytes 262176 | tf_op jit(solution)/shard_map/all_to_all | solution.py:218
  101.0 4.0 %all-to-all-start.2 = ((bf16[4,128,128]{1,2,0:T(8,128)(2,1)}), bf16[4,128,128]{1,2,0:T(8,128)(2,1)S(1)}, u32[]{:S(2)}, u32[]{:S(2)}) async-start(bf16[4,128,128]{1,2,0:T(8,128)(2,1)} %copy.42), calls=%async_computation.2 | async-start | bytes 262144 | tf_op jit(solution)/shard_map/all_to_all | solution.py:207
  105.1 0.1 add_add_fusion.1
  105.3 1.6 copy-done
  107.0 1.2 multiply_reduce_fusion
  108.2 0.3 fusion.94
  108.6 1.3 fusion.75
  109.8 1.9 collective-permute-start.3
  111.8 4.1 %collective-permute-start.2 = (bf16[1,1,8,16,1024]{4,3,2,1,0:T(8,128)(2,1)S(1)}, bf16[1,1,8,16,1024]{4,3,2,1,0:T(8,128)(2,1)S(1)}, u32[]{:S(2)}, u32[]{:S(2)}) collective-permute-start(bf16[1,1,8,16,1024]{4,3,2,1,0:T(8,128)(2,1)S(1)} %bitcast.245), channel_id=1, source_target_pairs={{0,4},{4,8},{8,12},{1,5},{5,9},{9,13},{2,6},{6,10},{10,14},{3,7},{... | collective-permute-start | bytes 786440 | tf_op jit(solution)/shard_map/ppermute | solution.py:18
  115.9 1.6 fusion.76
  117.5 2.6 %stack.130 = f32[27,1024]{1,0:T(8,128)} concatenate(f32[1,1024]{1,0:T(1,128)S(1)} %bitcast.331, f32[1,1024]{1,0:T(1,128)S(1)} %bitcast.332, f32[1,1024]{1,0:T(1,128)S(1)} %bitcast.333, f32[1,1024]{1,0:T(1,128)S(1)} %bitcast.334, f32[1,1024]{1,0:T(1,128)S(1)} %bitcast.329, f32[1,1024]{1,0:T(1,128)S(1)} %bitcast.335, f32[1,1024]{1,0:T(1,128)S(1)} %bitcast.336, ...), dimensions={0} | concatenate | bytes 221184 | tf_op jit(solution)/shard_map/stack | solution.py:68
  120.4 1.0 fusion.3
  121.5 88.4 %all-reduce.8.cloned.1.call-done = f32[27,1024]{1,0:T(8,128)} async-done(((f32[27,1024]{1,0:T(8,128)}), f32[27,1024]{1,0:T(8,128)}) %all-reduce.8.cloned.1.call-update) | async-done | bytes 110608 | tf_op jit(solution)/shard_map/psum | solution.py:261
  209.9 1.6 broadcast_multiply_fusion
  211.4 0.1 maximum_bitcast_fusion.1
  211.8 3.0 %fusion.90 = bf16[1,1,8,16,1024]{4,3,2,1,0:T(8,128)(2,1)} fusion(bf16[3,8,16,1024]{3,2,1,0:T(8,128)(2,1)S(1)} %maximum_bitcast_fusion.1, f32[1024]{0:T(1024)S(1)} %bitcast.280, f32[1024]{0:T(1024)S(1)} %bitcast.264, f32[1024]{0:T(1024)S(1)} %bitcast.274, f32[1024]{0:T(1024)S(1)} %bitcast.272, bf16[1,1,8,16,1024]{4,3,2,1,0:T(8,128)(2,1)S(1)} %collective-permute-done.3, ...), kind=kLoop, calls=%fused_computation.227 | loop fusion | flops 10747904 | bytes 1945600 | tf_op jit(solution)/shard_map/reshape | solution.py:262
  (171 shorter events, 1.3 us)
Async XLA Ops:
  7.2 21.9 %all-gather.4.cloned.1.call-start = ((), (), s32[]{:S(2)}) async-start(), calls=%async_computation.6 | async-start | bytes 2359296 | tf_op jit(solution)/shard_map/all_gather | solution.py:134
  9.5 23.0 %all-gather.8.cloned.1.call-start = ((), (), s32[]{:S(2)}) async-start(), calls=%async_computation.8 | async-start | bytes 1572864 | tf_op jit(solution)/shard_map/all_gather | solution.py:133
  10.3 37.2 %all-gather.6.cloned.1.call-start = ((), (), s32[]{:S(2)}) async-start(), calls=%async_computation.7 | async-start | bytes 4718592 | tf_op jit(solution)/shard_map/all_gather | solution.py:132
  11.0 9.9 %collective-permute-start = (bf16[1,1,8,16,1024]{4,3,2,1,0:T(8,128)(2,1)S(1)}, bf16[1,1,8,16,1024]{4,3,2,1,0:T(8,128)(2,1)S(1)}, u32[]{:S(2)}, u32[]{:S(2)}) collective-permute-start(bf16[1,1,8,16,1024]{4,3,2,1,0:T(8,128)(2,1)S(1)} %copy-done.6), channel_id=1, source_target_pairs={{0,4},{4,8},{8,12},{1,5},{5,9},{9,13},{2,6},{6,10},{10,14},{3,7},{... | collective-permute-start | bytes 786440 | tf_op jit(solution)/shard_map/ppermute | solution.py:18
  14.5 9.7 %collective-permute-start.1 = (bf16[1,1,8,16,1024]{4,3,2,1,0:T(8,128)(2,1)S(1)}, bf16[1,1,8,16,1024]{4,3,2,1,0:T(8,128)(2,1)S(1)}, u32[]{:S(2)}, u32[]{:S(2)}) collective-permute-start(bf16[1,1,8,16,1024]{4,3,2,1,0:T(8,128)(2,1)S(1)} %copy-done.6), channel_id=1, source_target_pairs={{4,0},{8,4},{12,8},{5,1},{9,5},{13,9},{6,2},{10,6},{14,10},{7,3},{... | collective-permute-start | bytes 786440 | tf_op jit(solution)/shard_map/ppermute | solution.py:19
  17.7 10.3 %copy-start.15 = (f32[1,1024]{1,0:T(1,128)}, f32[1,1024]{1,0:T(1,128)S(1)}, u32[]{:S(2)}) copy-start(f32[1,1024]{1,0:T(1,128)S(1)} %get-tuple-element.86) | copy-start | bytes 12292
  17.7 10.3 %copy-start.17 = (f32[1,1024]{1,0:T(1,128)}, f32[1,1024]{1,0:T(1,128)S(1)}, u32[]{:S(2)}) copy-start(f32[1,1024]{1,0:T(1,128)S(1)} %get-tuple-element.87) | copy-start | bytes 12292
  17.7 10.3 %copy-start.19 = (f32[1,1024]{1,0:T(1,128)}, f32[1,1024]{1,0:T(1,128)S(1)}, u32[]{:S(2)}) copy-start(f32[1,1024]{1,0:T(1,128)S(1)} %get-tuple-element.88) | copy-start | bytes 12292
  17.7 10.3 %copy-start.21 = (f32[1,1024]{1,0:T(1,128)}, f32[1,1024]{1,0:T(1,128)S(1)}, u32[]{:S(2)}) copy-start(f32[1,1024]{1,0:T(1,128)S(1)} %get-tuple-element.89) | copy-start | bytes 12292
  17.7 10.3 %copy-start.23 = (f32[1,1024]{1,0:T(1,128)}, f32[1,1024]{1,0:T(1,128)S(1)}, u32[]{:S(2)}) copy-start(f32[1,1024]{1,0:T(1,128)S(1)} %get-tuple-element.90) | copy-start | bytes 12292
  17.8 10.2 %copy-start.25 = (f32[1,1024]{1,0:T(1,128)}, f32[1,1024]{1,0:T(1,128)S(1)}, u32[]{:S(2)}) copy-start(f32[1,1024]{1,0:T(1,128)S(1)} %get-tuple-element.64) | copy-start | bytes 12292
  17.8 10.2 %copy-start.27 = (f32[1,1024]{1,0:T(1,128)}, f32[1,1024]{1,0:T(1,128)S(1)}, u32[]{:S(2)}) copy-start(f32[1,1024]{1,0:T(1,128)S(1)} %get-tuple-element.65) | copy-start | bytes 12292
  17.8 10.2 %copy-start.29 = (f32[1,1024]{1,0:T(1,128)}, f32[1,1024]{1,0:T(1,128)S(1)}, u32[]{:S(2)}) copy-start(f32[1,1024]{1,0:T(1,128)S(1)} %get-tuple-element.66) | copy-start | bytes 12292
  17.8 10.2 %copy-start.31 = (f32[1,1024]{1,0:T(1,128)}, f32[1,1024]{1,0:T(1,128)S(1)}, u32[]{:S(2)}) copy-start(f32[1,1024]{1,0:T(1,128)S(1)} %get-tuple-element.67) | copy-start | bytes 12292
  17.8 10.2 %copy-start.33 = (f32[1,1024]{1,0:T(1,128)}, f32[1,1024]{1,0:T(1,128)S(1)}, u32[]{:S(2)}) copy-start(f32[1,1024]{1,0:T(1,128)S(1)} %get-tuple-element.68) | copy-start | bytes 12292
  17.9 10.2 %copy-start.35 = (f32[1,1024]{1,0:T(1,128)}, f32[1,1024]{1,0:T(1,128)S(1)}, u32[]{:S(2)}) copy-start(f32[1,1024]{1,0:T(1,128)S(1)} %get-tuple-element.69) | copy-start | bytes 12292
  17.9 10.2 %copy-start.37 = (f32[1,1024]{1,0:T(1,128)}, f32[1,1024]{1,0:T(1,128)S(1)}, u32[]{:S(2)}) copy-start(f32[1,1024]{1,0:T(1,128)S(1)} %get-tuple-element.70) | copy-start | bytes 12292
  17.9 10.2 %copy-start.39 = (f32[1,1024]{1,0:T(1,128)}, f32[1,1024]{1,0:T(1,128)S(1)}, u32[]{:S(2)}) copy-start(f32[1,1024]{1,0:T(1,128)S(1)} %get-tuple-element.71) | copy-start | bytes 12292
  17.9 10.2 %copy-start.41 = (f32[1,1024]{1,0:T(1,128)}, f32[1,1024]{1,0:T(1,128)S(1)}, u32[]{:S(2)}) copy-start(f32[1,1024]{1,0:T(1,128)S(1)} %get-tuple-element.72) | copy-start | bytes 12292
  17.9 10.2 %copy-start.43 = (f32[1,1024]{1,0:T(1,128)}, f32[1,1024]{1,0:T(1,128)S(1)}, u32[]{:S(2)}) copy-start(f32[1,1024]{1,0:T(1,128)S(1)} %get-tuple-element.73) | copy-start | bytes 12292
  17.9 10.2 %copy-start.45 = (f32[1,1024]{1,0:T(1,128)}, f32[1,1024]{1,0:T(1,128)S(1)}, u32[]{:S(2)}) copy-start(f32[1,1024]{1,0:T(1,128)S(1)} %get-tuple-element.74) | copy-start | bytes 12292
  17.9 10.2 %copy-start.47 = (f32[1,1024]{1,0:T(1,128)}, f32[1,1024]{1,0:T(1,128)S(1)}, u32[]{:S(2)}) copy-start(f32[1,1024]{1,0:T(1,128)S(1)} %get-tuple-element.75) | copy-start | bytes 12292
  17.9 10.2 %copy-start.49 = (f32[1,1024]{1,0:T(1,128)}, f32[1,1024]{1,0:T(1,128)S(1)}, u32[]{:S(2)}) copy-start(f32[1,1024]{1,0:T(1,128)S(1)} %get-tuple-element.76) | copy-start | bytes 12292
  17.9 10.2 %copy-start.51 = (f32[1,1024]{1,0:T(1,128)}, f32[1,1024]{1,0:T(1,128)S(1)}, u32[]{:S(2)}) copy-start(f32[1,1024]{1,0:T(1,128)S(1)} %get-tuple-element.77) | copy-start | bytes 12292
  17.9 10.2 %copy-start.53 = (f32[1,1024]{1,0:T(1,128)}, f32[1,1024]{1,0:T(1,128)S(1)}, u32[]{:S(2)}) copy-start(f32[1,1024]{1,0:T(1,128)S(1)} %get-tuple-element.78) | copy-start | bytes 12292
  18.0 10.2 %copy-start.55 = (f32[1,1024]{1,0:T(1,128)}, f32[1,1024]{1,0:T(1,128)S(1)}, u32[]{:S(2)}) copy-start(f32[1,1024]{1,0:T(1,128)S(1)} %get-tuple-element.79) | copy-start | bytes 12292
  31.1 16.4 %copy-start.63 = (f32[1,1,1024]{2,0,1:T(1,128)}, f32[1,1,1024]{2,0,1:T(1,128)S(1)}, u32[]{:S(2)}) copy-start(f32[1,1,1024]{2,0,1:T(1,128)S(1)} %get-tuple-element.91) | copy-start | bytes 12292
  31.1 16.4 %copy-start.65 = (f32[1,1,1024]{2,0,1:T(1,128)}, f32[1,1,1024]{2,0,1:T(1,128)S(1)}, u32[]{:S(2)}) copy-start(f32[1,1,1024]{2,0,1:T(1,128)S(1)} %get-tuple-element.93) | copy-start | bytes 12292
  35.1 19.2 %all-to-all-start.3 = ((bf16[4,128,128]{1,2,0:T(8,128)(2,1)}), bf16[4,128,128]{1,2,0:T(8,128)(2,1)S(1)}, u32[]{:S(2)}, u32[]{:S(2)}) async-start(bf16[4,128,128]{1,2,0:T(8,128)(2,1)} %bitcast.65), calls=%async_computation.3 | async-start | bytes 262144 | tf_op jit(solution)/shard_map/all_to_all | solution.py:179
  54.2 10.4 %all-to-all-start.1 = ((bf16[4,128,128]{1,2,0:T(8,128)(2,1)}), bf16[4,128,128]{1,2,0:T(8,128)(2,1)S(1)}, u32[]{:S(2)}, u32[]{:S(2)}) async-start(bf16[4,128,128]{1,2,0:T(8,128)(2,1)} %bitcast.54), calls=%async_computation.1 | async-start | bytes 262144 | tf_op jit(solution)/shard_map/all_to_all | solution.py:176
  64.6 10.8 %all-to-all-start = ((bf16[4,128,256]{1,2,0:T(8,128)(2,1)}), bf16[4,128,256]{1,2,0:T(8,128)(2,1)S(1)}, u32[]{:S(2)}, u32[]{:S(2)}) async-start(bf16[4,128,256]{1,2,0:T(8,128)(2,1)} %bitcast.50), calls=%async_computation | async-start | bytes 524288 | tf_op jit(solution)/shard_map/all_to_all | solution.py:195
  79.4 11.5 %all-to-all-start.4 = ((bf16[4,128,256]{1,2,0:T(8,128)(2,1)}), bf16[4,128,256]{1,2,0:T(8,128)(2,1)S(1)}, u32[]{:S(2)}, u32[]{:S(2)}) async-start(bf16[4,128,256]{1,2,0:T(8,128)(2,1)} %copy.48), calls=%async_computation.4 | async-start | bytes 524288 | tf_op jit(solution)/shard_map/all_to_all | solution.py:227
  85.9 19.1 %copy-start.4 = (f32[128,3,8,64]{0,3,2,1:T(8,128)S(1)}, f32[128,3,8,64]{0,3,2,1:T(8,128)}, u32[]{:S(2)}) copy-start(f32[128,3,8,64]{0,3,2,1:T(8,128)} %copy-done.3) | copy-start | bytes 2359300
  90.8 10.2 %all-to-all-start.5 = ((f32[4,128,128]{1,2,0:T(8,128)}), f32[4,128,128]{1,2,0:T(8,128)S(1)}, u32[]{:S(2)}, u32[]{:S(2)}) async-start(f32[4,128,128]{1,2,0:T(8,128)} %copy.50), calls=%async_computation.5 | async-start | bytes 524288 | tf_op jit(solution)/shard_map/all_to_all | solution.py:218
  101.0 19.1 %all-to-all-start.2 = ((bf16[4,128,128]{1,2,0:T(8,128)(2,1)}), bf16[4,128,128]{1,2,0:T(8,128)(2,1)S(1)}, u32[]{:S(2)}, u32[]{:S(2)}) async-start(bf16[4,128,128]{1,2,0:T(8,128)(2,1)} %copy.42), calls=%async_computation.2 | async-start | bytes 262144 | tf_op jit(solution)/shard_map/all_to_all | solution.py:207
  105.0 104.8 %all-reduce.8.cloned.1.call-start = ((), (), s32[]{:S(2)}) async-start(), calls=%async_computation.9 | async-start | bytes 262144 | tf_op jit(solution)/shard_map/psum | solution.py:261
  108.5 11.6 %copy-start.5 = (bf16[512,1024]{1,0:T(8,128)(2,1)S(1)}, bf16[512,1024]{1,0:T(8,128)(2,1)}, u32[]{:S(2)}) copy-start(bf16[512,1024]{1,0:T(8,128)(2,1)} %all-gather.8.cloned.1.call-done) | copy-start | bytes 3145732
  108.5 11.6 %copy-start.64 = (f32[1,1,1024]{2,0,1:T(1,128)S(1)}, f32[1,1,1024]{2,0,1:T(1,128)}, u32[]{:S(2)}) copy-start(f32[1,1,1024]{2,0,1:T(1,128)} %copy-done.63) | copy-start | bytes 12292
  109.8 101.6 %collective-permute-start.3 = (bf16[1,1,8,16,1024]{4,3,2,1,0:T(8,128)(2,1)S(1)}, bf16[1,1,8,16,1024]{4,3,2,1,0:T(8,128)(2,1)S(1)}, u32[]{:S(2)}, u32[]{:S(2)}) collective-permute-start(bf16[1,1,8,16,1024]{4,3,2,1,0:T(8,128)(2,1)S(1)} %bitcast.244), channel_id=1, source_target_pairs={{4,0},{8,4},{12,8},{5,1},{9,5},{13,9},{6,2},{10,6},{14,10},{7,3},{... | collective-permute-start | bytes 786440 | tf_op jit(solution)/shard_map/ppermute | solution.py:19
  111.8 99.7 %collective-permute-start.2 = (bf16[1,1,8,16,1024]{4,3,2,1,0:T(8,128)(2,1)S(1)}, bf16[1,1,8,16,1024]{4,3,2,1,0:T(8,128)(2,1)S(1)}, u32[]{:S(2)}, u32[]{:S(2)}) collective-permute-start(bf16[1,1,8,16,1024]{4,3,2,1,0:T(8,128)(2,1)S(1)} %bitcast.245), channel_id=1, source_target_pairs={{0,4},{4,8},{8,12},{1,5},{5,9},{9,13},{2,6},{6,10},{10,14},{3,7},{... | collective-permute-start | bytes 786440 | tf_op jit(solution)/shard_map/ppermute | solution.py:18
  120.2 91.3 %copy-start.16 = (f32[1,1024]{1,0:T(1,128)S(1)}, f32[1,1024]{1,0:T(1,128)}, u32[]{:S(2)}) copy-start(f32[1,1024]{1,0:T(1,128)} %copy-done.15) | copy-start | bytes 12292
  120.2 91.3 %copy-start.18 = (f32[1,1024]{1,0:T(1,128)S(1)}, f32[1,1024]{1,0:T(1,128)}, u32[]{:S(2)}) copy-start(f32[1,1024]{1,0:T(1,128)} %copy-done.17) | copy-start | bytes 12292
  120.2 91.3 %copy-start.20 = (f32[1,1024]{1,0:T(1,128)S(1)}, f32[1,1024]{1,0:T(1,128)}, u32[]{:S(2)}) copy-start(f32[1,1024]{1,0:T(1,128)} %copy-done.19) | copy-start | bytes 12292
  120.2 91.3 %copy-start.22 = (f32[1,1024]{1,0:T(1,128)S(1)}, f32[1,1024]{1,0:T(1,128)}, u32[]{:S(2)}) copy-start(f32[1,1024]{1,0:T(1,128)} %copy-done.21) | copy-start | bytes 12292
  120.2 91.3 %copy-start.24 = (f32[1,1024]{1,0:T(1,128)S(1)}, f32[1,1024]{1,0:T(1,128)}, u32[]{:S(2)}) copy-start(f32[1,1024]{1,0:T(1,128)} %copy-done.23) | copy-start | bytes 12292
  120.2 91.3 %copy-start.26 = (f32[1,1024]{1,0:T(1,128)S(1)}, f32[1,1024]{1,0:T(1,128)}, u32[]{:S(2)}) copy-start(f32[1,1024]{1,0:T(1,128)} %copy-done.25) | copy-start | bytes 12292
  120.3 91.3 %copy-start.28 = (f32[1,1024]{1,0:T(1,128)S(1)}, f32[1,1024]{1,0:T(1,128)}, u32[]{:S(2)}) copy-start(f32[1,1024]{1,0:T(1,128)} %copy-done.27) | copy-start | bytes 12292
  120.3 91.3 %copy-start.30 = (f32[1,1024]{1,0:T(1,128)S(1)}, f32[1,1024]{1,0:T(1,128)}, u32[]{:S(2)}) copy-start(f32[1,1024]{1,0:T(1,128)} %copy-done.29) | copy-start | bytes 12292
  120.3 91.3 %copy-start.32 = (f32[1,1024]{1,0:T(1,128)S(1)}, f32[1,1024]{1,0:T(1,128)}, u32[]{:S(2)}) copy-start(f32[1,1024]{1,0:T(1,128)} %copy-done.31) | copy-start | bytes 12292
  120.3 91.3 %copy-start.34 = (f32[1,1024]{1,0:T(1,128)S(1)}, f32[1,1024]{1,0:T(1,128)}, u32[]{:S(2)}) copy-start(f32[1,1024]{1,0:T(1,128)} %copy-done.33) | copy-start | bytes 12292
  120.3 91.3 %copy-start.36 = (f32[1,1024]{1,0:T(1,128)S(1)}, f32[1,1024]{1,0:T(1,128)}, u32[]{:S(2)}) copy-start(f32[1,1024]{1,0:T(1,128)} %copy-done.35) | copy-start | bytes 12292
  120.3 91.3 %copy-start.38 = (f32[1,1024]{1,0:T(1,128)S(1)}, f32[1,1024]{1,0:T(1,128)}, u32[]{:S(2)}) copy-start(f32[1,1024]{1,0:T(1,128)} %copy-done.37) | copy-start | bytes 12292
  120.3 91.3 %copy-start.40 = (f32[1,1024]{1,0:T(1,128)S(1)}, f32[1,1024]{1,0:T(1,128)}, u32[]{:S(2)}) copy-start(f32[1,1024]{1,0:T(1,128)} %copy-done.39) | copy-start | bytes 12292
  120.3 91.3 %copy-start.42 = (f32[1,1024]{1,0:T(1,128)S(1)}, f32[1,1024]{1,0:T(1,128)}, u32[]{:S(2)}) copy-start(f32[1,1024]{1,0:T(1,128)} %copy-done.41) | copy-start | bytes 12292
  120.3 91.3 %copy-start.44 = (f32[1,1024]{1,0:T(1,128)S(1)}, f32[1,1024]{1,0:T(1,128)}, u32[]{:S(2)}) copy-start(f32[1,1024]{1,0:T(1,128)} %copy-done.43) | copy-start | bytes 12292
  120.3 91.3 %copy-start.46 = (f32[1,1024]{1,0:T(1,128)S(1)}, f32[1,1024]{1,0:T(1,128)}, u32[]{:S(2)}) copy-start(f32[1,1024]{1,0:T(1,128)} %copy-done.45) | copy-start | bytes 12292
  120.4 91.3 %copy-start.48 = (f32[1,1024]{1,0:T(1,128)S(1)}, f32[1,1024]{1,0:T(1,128)}, u32[]{:S(2)}) copy-start(f32[1,1024]{1,0:T(1,128)} %copy-done.47) | copy-start | bytes 12292
  120.4 91.3 %copy-start.50 = (f32[1,1024]{1,0:T(1,128)S(1)}, f32[1,1024]{1,0:T(1,128)}, u32[]{:S(2)}) copy-start(f32[1,1024]{1,0:T(1,128)} %copy-done.49) | copy-start | bytes 12292
  120.4 91.3 %copy-start.52 = (f32[1,1024]{1,0:T(1,128)S(1)}, f32[1,1024]{1,0:T(1,128)}, u32[]{:S(2)}) copy-start(f32[1,1024]{1,0:T(1,128)} %copy-done.51) | copy-start | bytes 12292
  120.4 91.3 %copy-start.54 = (f32[1,1024]{1,0:T(1,128)S(1)}, f32[1,1024]{1,0:T(1,128)}, u32[]{:S(2)}) copy-start(f32[1,1024]{1,0:T(1,128)} %copy-done.53) | copy-start | bytes 12292
  120.4 91.3 %copy-start.56 = (f32[1,1024]{1,0:T(1,128)S(1)}, f32[1,1024]{1,0:T(1,128)}, u32[]{:S(2)}) copy-start(f32[1,1024]{1,0:T(1,128)} %copy-done.55) | copy-start | bytes 12292
  120.4 91.3 %copy-start.58 = (f32[1,1024]{1,0:T(1,128)S(1)}, f32[1,1024]{1,0:T(1,128)}, u32[]{:S(2)}) copy-start(f32[1,1024]{1,0:T(1,128)} %copy-done.57) | copy-start | bytes 12292
  120.4 91.3 %copy-start.60 = (f32[1,1024]{1,0:T(1,128)S(1)}, f32[1,1024]{1,0:T(1,128)}, u32[]{:S(2)}) copy-start(f32[1,1024]{1,0:T(1,128)} %copy-done.59) | copy-start | bytes 12292
  120.4 91.3 %copy-start.62 = (f32[1,1024]{1,0:T(1,128)S(1)}, f32[1,1024]{1,0:T(1,128)}, u32[]{:S(2)}) copy-start(f32[1,1024]{1,0:T(1,128)} %copy-done.61) | copy-start | bytes 12292
  (19 other events, 84.6 us)
Sparse Core Ops, SparseCore 0:
  9.7 11.0 all-gather.3
  22.3 10.1 all-gather.7
  34.1 13.2 all-gather.5
  120.3 89.5 all-reduce.7
where the time goes:
time: 222 us; the launch traced here: 221 us
  waiting for transfers between devices  124 us (56%)
  starting transfers between devices  40 us (18%)
  local copies, waits for them, and re-layouts  17.4 us (8%)
  between operations  15.6 us (7%)
  other arithmetic  13.9 us (6%)
  matrix products  10.6 us (5%)
    psum x1, waiting for transfers between devices, shards(): grad_kernel = lax.psum(local_terms, ('seq', 'dp', 'fsdp')) * norm_factor  88.4 us
    ppermute x2, starting transfers between devices, padded_2(): before = lax.ppermute(last, axis, up)  7.59 us
    all_gather x1, waiting for transfers between devices, shards(): lax.all_gather(qkv_weight, 'fsdp', axis=0, tiled=True)  6.31 us
    all_to_all x1, waiting for transfers between devices, shards(): lax.all_to_all(dquery.reshape(seq_count, part_rows, group_width), 'seq',...  6.13 us
    all_to_all x1, waiting for transfers between devices, shards(): lax.all_to_all(copies.reshape(seq_count, row_count, 2 * group_width), 'se...  5.98 us
    unnamed x139, local copies, waits for them, and re-layouts  5.94 us
    all_to_all x1, starting transfers between devices, shards(): lax.all_to_all(grads_kv.reshape(seq_count, row_count, 2 * group_width).as...  5.23 us
    all_to_all x1, starting transfers between devices, shards(): lax.all_to_all(to_heads(grad_attn), 'seq', split_axis=0, concat_axis=0, t...  5.16 us
  transfers between devices with their start and end apart: 14, of which 9 were waited for; matrix products, arithmetic and copies ran while one was open for 13% of the time, Pallas kernels for 0%

commit v1 on v0

--- a/solution.py
+++ b/solution.py
@@ -258,7 +258,11 @@
     norm_factor = 1.0 / math.sqrt(
         lax.axis_size("dp") * lax.axis_size("fsdp") * seq_count * row_count
     )
-    grad_kernel = lax.psum(local_terms, ("seq", "dp", "fsdp")) * norm_factor
+
+    def time_the_samples(shard_in):
+        return jax.lax.all_gather(shard_in, ("seq", "dp", "fsdp")).sum(axis=0)
+
+    grad_kernel = time_the_samples(local_terms) * norm_factor
     return (out_rows.reshape(tokens.shape), grad_tokens.reshape(tokens.shape), grad_kernel)
 
 

time: 222 us -> 166 us (0.75)
  the two profiles are of different devices: /device:TPU:8 before, /device:TPU:0 now
where the time goes in v1:
time: 166 us; the launch traced here: 165 us
  waiting for transfers between devices  66.6 us (40%)
  starting transfers between devices  36.4 us (22%)
  other arithmetic  18.1 us (11%)
  local copies, waits for them, and re-layouts  17.6 us (11%)
  between operations  15.8 us (10%)
  matrix products  10.6 us (6%)
    all_gather x1, waiting for transfers between devices, time_the_samples(): return jax.lax.all_gather(shard_in, ('seq', 'dp', 'fsdp')).sum(axis=0)  23.1 us
    ppermute x2, starting transfers between devices, padded_2(): before = lax.ppermute(last, axis, up)  9.52 us
    all_to_all x1, waiting for transfers between devices, shards(): lax.all_to_all(copies.reshape(seq_count, row_count, 2 * group_width), 'se...  7.8 us
    ppermute x2, waiting for transfers between devices, padded_2(): after = lax.ppermute(leading, axis, down)  7.08 us
    all_gather x1, waiting for transfers between devices, shards(): lax.all_gather(qkv_weight, 'fsdp', axis=0, tiled=True)  6.6 us
    all_to_all x1, waiting for transfers between devices, shards(): lax.all_to_all(dquery.reshape(seq_count, part_rows, group_width), 'seq',...  5.71 us
    all_to_all x1, starting transfers between devices, shards(): lax.all_to_all(to_heads(query_f.astype(jnp.bfloat16)), 'seq', split_axis=...  4.86 us
    all_to_all x1, starting transfers between devices, shards(): lax.all_to_all(to_heads(grad_attn), 'seq', split_axis=0, concat_axis=0, t...  4.85 us
  transfers between devices with their start and end apart: 14, of which 12 were waited for; matrix products, arithmetic and copies ran while one was open for 15% of the time, Pallas kernels for 0%

profile of v1, /device:TPU:0, one launch (start us, length us, event | category | flops | bytes accessed | tf_op | source)
XLA Modules:
  0.0 165.2 jit_solution(7648555025534904395)
XLA Ops:
  7.2 2.3 %copy.35 = bf16[128,3072]{0,1:T(8,128)(2,1)} copy(bf16[128,3072]{1,0:T(8,128)(2,1)} %param.11) | data formatting | bytes 1572864 | tf_op args[3]
  9.6 0.7 all-gather.11.cloned.1.call-update
  10.4 0.7 all-gather.9.cloned.1.call-update
  11.1 4.9 %collective-permute-start = (bf16[1,1,8,16,1024]{4,3,2,1,0:T(8,128)(2,1)S(1)}, bf16[1,1,8,16,1024]{4,3,2,1,0:T(8,128)(2,1)S(1)}, u32[]{:S(2)}, u32[]{:S(2)}) collective-permute-start(bf16[1,1,8,16,1024]{4,3,2,1,0:T(8,128)(2,1)S(1)} %copy-done.5), channel_id=1, source_target_pairs={{0,4},{4,8},{8,12},{1,5},{5,9},{9,13},{2,6},{6,10},{10,14},{3,7},{... | collective-permute-start | bytes 786440 | tf_op jit(solution)/shard_map/ppermute | solution.py:18
  16.0 1.3 collective-permute-start.1
  18.5 3.1 %collective-permute-done = bf16[1,1,8,16,1024]{4,3,2,1,0:T(8,128)(2,1)S(1)} collective-permute-done((bf16[1,1,8,16,1024]{4,3,2,1,0:T(8,128)(2,1)S(1)}, bf16[1,1,8,16,1024]{4,3,2,1,0:T(8,128)(2,1)S(1)}, u32[]{:S(2)}, u32[]{:S(2)}) %collective-permute-start) | collective-permute-done | bytes 262176 | tf_op jit(solution)/shard_map/ppermute | solution.py:18
  21.6 4.1 %collective-permute-done.1 = bf16[1,1,8,16,1024]{4,3,2,1,0:T(8,128)(2,1)S(1)} collective-permute-done((bf16[1,1,8,16,1024]{4,3,2,1,0:T(8,128)(2,1)S(1)}, bf16[1,1,8,16,1024]{4,3,2,1,0:T(8,128)(2,1)S(1)}, u32[]{:S(2)}, u32[]{:S(2)}) %collective-permute-start.1) | collective-permute-done | bytes 262176 | tf_op jit(solution)/shard_map/ppermute | solution.py:19
  25.8 0.9 copy-done.1
  26.7 2.7 %convert_reduce_fusion = (f32[8,16]{1,0:T(8,128)S(1)}, bf16[1,8,16,1024]{3,2,1,0:T(8,128)(2,1)S(1)}) fusion(f32[1024]{0:T(1024)S(1)} %bitcast.275, f32[1024]{0:T(1024)S(1)} %bitcast.277, f32[1024]{0:T(1024)S(1)} %bitcast.281, f32[1024]{0:T(1024)S(1)} %bitcast.283, bf16[1,1,8,16,1024]{4,3,2,1,0:T(8,128)(2,1)S(1)} %collective-permute-done.1, ...), kind=kLoop, calls=%fused_computation.221 | loop fusion | flops 11009920 | bytes 1946112 | tf_op jit(solution)/shard_map/reduce_sum | solution.py:72
  29.9 0.6 multiply_add_fusion.1
  30.5 2.0 %fusion.103 = f32[1,3,1024]{2,0,1:T(1,128)S(1)} fusion(bf16[256,1,1]{0,1,2:T(2,128)(2,1)S(1)} %reshape.540, bf16[3,1024,256]{2,1,0:T(8,128)(2,1)} %bitcast.251), kind=kOutput, calls=%fused_computation.254 | convolution fusion | flops 1572864 | bytes 1585664 | tf_op jit(solution)/shard_map/dot_general | solution.py:34
  32.6 1.3 all-gather.11.cloned.1.call-done
  34.0 1.7 %convolution_convert_fusion.2 = bf16[128,512]{1,0:T(8,128)(2,1)S(1)} fusion(bf16[512,1024]{1,0:T(8,128)(2,1)} %all-gather.11.cloned.1.call-done, bf16[128,1024]{1,0:T(8,128)(2,1)S(1)} %bitcast.255, f32[1024]{0:T(1024)S(1)} %bitcast.317), kind=kOutput, calls=%fused_computation.88 | convolution fusion | flops 134676480 | bytes 1445888 | tf_op jit(solution)/shard_map/dot_general | solution.py:163
  35.7 0.8 copy.58
  36.4 4.9 %all-to-all-start.3 = ((bf16[4,128,128]{1,2,0:T(8,128)(2,1)}), bf16[4,128,128]{1,2,0:T(8,128)(2,1)S(1)}, u32[]{:S(2)}, u32[]{:S(2)}) async-start(bf16[4,128,128]{1,2,0:T(8,128)(2,1)} %bitcast.65), calls=%async_computation.3 | async-start | bytes 262144 | tf_op jit(solution)/shard_map/all_to_all | solution.py:179
  41.3 0.9 add_convert_fusion.1
  42.2 6.6 %all-gather.9.cloned.1.call-done = bf16[1024,1536]{1,0:T(8,128)(2,1)} async-done(((bf16[512,1536]{1,0:T(8,128)(2,1)}), bf16[1024,1536]{1,0:T(8,128)(2,1)}) %all-gather.9.cloned.1.call-update) | async-done | bytes 3145744 | tf_op jit(solution)/shard_map/all_gather | solution.py:132
  48.8 3.2 %copy.36 = bf16[1536,1024]{1,0:T(8,128)(2,1)S(1)} copy(bf16[1536,1024]{0,1:T(8,128)(2,1)} %bitcast.243) | data formatting | bytes 6291456 | tf_op jit(solution)/shard_map/dot_general | solution.py:159
  52.0 1.9 %fusion.104 = f32[128,3,8,64]{0,3,2,1:T(8,128)S(1)} fusion(bf16[128,1024,1,1]{1,0,3,2:T(8,128)(2,1)} %bitcast.254, bf16[3,8,64,1024]{3,2,1,0:T(8,128)(2,1)S(1)} %bitcast.244), kind=kOutput, calls=%fused_computation.255 | convolution fusion | flops 402653184 | bytes 4194304 | tf_op jit(solution)/shard_map/dot_general | solution.py:159
  54.0 0.8 copy-done.3
  54.9 0.7 fusion.98
  55.6 4.9 %all-to-all-start.1 = ((bf16[4,128,128]{1,2,0:T(8,128)(2,1)}), bf16[4,128,128]{1,2,0:T(8,128)(2,1)S(1)}, u32[]{:S(2)}, u32[]{:S(2)}) async-start(bf16[4,128,128]{1,2,0:T(8,128)(2,1)} %bitcast.54), calls=%async_computation.1 | async-start | bytes 262144 | tf_op jit(solution)/shard_map/all_to_all | solution.py:176
  60.4 1.0 slice.712
  61.4 0.7 pad_maximum_fusion
  62.1 4.7 %all-to-all-done.1 = bf16[4,128,128]{1,2,0:T(8,128)(2,1)S(1)} async-done(((bf16[4,128,128]{1,2,0:T(8,128)(2,1)}), bf16[4,128,128]{1,2,0:T(8,128)(2,1)S(1)}, u32[]{:S(2)}, u32[]{:S(2)}) %all-to-all-start.1) | async-done | bytes 131104 | tf_op jit(solution)/shard_map/all_to_all | solution.py:176
  66.8 3.4 %all-to-all-start = ((bf16[4,128,256]{1,2,0:T(8,128)(2,1)}), bf16[4,128,256]{1,2,0:T(8,128)(2,1)S(1)}, u32[]{:S(2)}, u32[]{:S(2)}) async-start(bf16[4,128,256]{1,2,0:T(8,128)(2,1)} %bitcast.50), calls=%async_computation | async-start | bytes 524288 | tf_op jit(solution)/shard_map/all_to_all | solution.py:195
  70.6 7.8 %all-to-all-done = bf16[4,128,256]{1,2,0:T(8,128)(2,1)S(1)} async-done(((bf16[4,128,256]{1,2,0:T(8,128)(2,1)}), bf16[4,128,256]{1,2,0:T(8,128)(2,1)S(1)}, u32[]{:S(2)}, u32[]{:S(2)}) %all-to-all-start) | async-done | bytes 262176 | tf_op jit(solution)/shard_map/all_to_all | solution.py:195
  78.4 0.2 copy.39
  78.7 0.5 fusion.1
  79.2 0.3 fusion.7
  79.6 0.4 fusion.6
  80.0 0.3 multiply_reduce_fusion.4
  80.3 0.7 multiply_convert_fusion
  81.0 0.4 fusion.5
  81.6 0.7 copy.48
  82.3 3.4 %all-to-all-start.4 = ((bf16[4,128,256]{1,2,0:T(8,128)(2,1)}), bf16[4,128,256]{1,2,0:T(8,128)(2,1)S(1)}, u32[]{:S(2)}, u32[]{:S(2)}) async-start(bf16[4,128,256]{1,2,0:T(8,128)(2,1)} %copy.48), calls=%async_computation.4 | async-start | bytes 524288 | tf_op jit(solution)/shard_map/all_to_all | solution.py:227
  85.8 0.6 div.54
  86.4 0.6 add.273
  86.9 0.3 convolution_bitcast_fusion
  87.3 0.7 copy.50
  88.1 4.4 %all-to-all-done.4 = bf16[4,128,256]{1,2,0:T(8,128)(2,1)S(1)} async-done(((bf16[4,128,256]{1,2,0:T(8,128)(2,1)}), bf16[4,128,256]{1,2,0:T(8,128)(2,1)S(1)}, u32[]{:S(2)}, u32[]{:S(2)}) %all-to-all-start.4) | async-done | bytes 262176 | tf_op jit(solution)/shard_map/all_to_all | solution.py:227
  92.5 4.0 %all-to-all-start.5 = ((f32[4,128,128]{1,2,0:T(8,128)}), f32[4,128,128]{1,2,0:T(8,128)}, u32[]{:S(2)}, u32[]{:S(2)}) async-start(f32[4,128,128]{1,2,0:T(8,128)} %copy.50), calls=%async_computation.5 | async-start | bytes 524288 | tf_op jit(solution)/shard_map/all_to_all | solution.py:218
  96.5 0.2 all-gather.13.cloned.1.call-start
  96.8 0.8 fusion.97
  97.7 5.7 %all-to-all-done.5 = f32[4,128,128]{1,2,0:T(8,128)} async-done(((f32[4,128,128]{1,2,0:T(8,128)}), f32[4,128,128]{1,2,0:T(8,128)}, u32[]{:S(2)}, u32[]{:S(2)}) %all-to-all-start.5) | async-done | bytes 262176 | tf_op jit(solution)/shard_map/all_to_all | solution.py:218
  103.4 1.3 multiply_reduce_fusion.1
  104.7 1.3 add_add_fusion.1
  106.0 1.0 add_convert_fusion
  107.1 1.2 multiply_reduce_fusion
  108.4 0.3 fusion.94
  108.7 1.3 fusion.75
  110.0 1.6 fusion.76
  111.6 2.6 %stack.130 = f32[27,1024]{1,0:T(8,128)} concatenate(f32[1,1024]{1,0:T(1,128)S(1)} %bitcast.331, f32[1,1024]{1,0:T(1,128)S(1)} %bitcast.332, f32[1,1024]{1,0:T(1,128)S(1)} %bitcast.333, f32[1,1024]{1,0:T(1,128)S(1)} %bitcast.334, f32[1,1024]{1,0:T(1,128)S(1)} %bitcast.329, f32[1,1024]{1,0:T(1,128)S(1)} %bitcast.335, f32[1,1024]{1,0:T(1,128)S(1)} %bitcast.336, ...), dimensions={0} | concatenate | bytes 221184 | tf_op jit(solution)/shard_map/stack | solution.py:68
  114.6 0.7 copy.42
  115.2 3.4 %all-to-all-start.2 = ((bf16[4,128,128]{1,2,0:T(8,128)(2,1)}), bf16[4,128,128]{1,2,0:T(8,128)(2,1)S(1)}, u32[]{:S(2)}, u32[]{:S(2)}) async-start(bf16[4,128,128]{1,2,0:T(8,128)(2,1)} %copy.42), calls=%async_computation.2 | async-start | bytes 262144 | tf_op jit(solution)/shard_map/all_to_all | solution.py:207
  118.7 1.3 collective-permute-start.3
  119.9 4.6 %collective-permute-start.2 = (bf16[1,1,8,16,1024]{4,3,2,1,0:T(8,128)(2,1)S(1)}, bf16[1,1,8,16,1024]{4,3,2,1,0:T(8,128)(2,1)S(1)}, u32[]{:S(2)}, u32[]{:S(2)}) collective-permute-start(bf16[1,1,8,16,1024]{4,3,2,1,0:T(8,128)(2,1)S(1)} %bitcast.246), channel_id=1, source_target_pairs={{0,4},{4,8},{8,12},{1,5},{5,9},{9,13},{2,6},{6,10},{10,14},{3,7},{... | collective-permute-start | bytes 786440 | tf_op jit(solution)/shard_map/ppermute | solution.py:18
  124.7 1.0 fusion.3
  125.7 3.0 %collective-permute-done.3 = bf16[1,1,8,16,1024]{4,3,2,1,0:T(8,128)(2,1)S(1)} collective-permute-done((bf16[1,1,8,16,1024]{4,3,2,1,0:T(8,128)(2,1)S(1)}, bf16[1,1,8,16,1024]{4,3,2,1,0:T(8,128)(2,1)S(1)}, u32[]{:S(2)}, u32[]{:S(2)}) %collective-permute-start.3) | collective-permute-done | bytes 262176 | tf_op jit(solution)/shard_map/ppermute | solution.py:19
  128.7 1.2 collective-permute-done.2
  130.2 2.9 %fusion.90 = bf16[1,1,8,16,1024]{4,3,2,1,0:T(8,128)(2,1)} fusion(bf16[3,8,16,1024]{3,2,1,0:T(8,128)(2,1)S(1)} %maximum_bitcast_fusion.1, f32[1024]{0:T(1024)S(1)} %bitcast.280, f32[1024]{0:T(1024)S(1)} %bitcast.264, f32[1024]{0:T(1024)S(1)} %bitcast.274, f32[1024]{0:T(1024)S(1)} %bitcast.272, bf16[1,1,8,16,1024]{4,3,2,1,0:T(8,128)(2,1)S(1)} %collective-permute-done.3, ...), kind=kLoop, calls=%fused_computation.227 | loop fusion | flops 10747904 | bytes 1945600 | tf_op jit(solution)/shard_map/reshape | solution.py:266
  133.2 23.1 %all-gather.13.cloned.1.call-done = f32[16,27,1024]{2,1,0:T(8,128)} async-done(((f32[1,27,1024]{2,1,0:T(8,128)}), f32[16,27,1024]{2,1,0:T(8,128)}) %all-gather.13.cloned.1.call-update) | async-done | bytes 1769488 | tf_op jit(solution)/shard_map/all_gather | solution.py:263
  156.3 1.7 %reduce_sum.389 = f32[27,1024]{1,0:T(8,128)S(1)} reduce(f32[16,27,1024]{2,1,0:T(8,128)} %all-gather.13.cloned.1.call-done, f32[]{:T(128)} %constant.17.clone.1), dimensions={0}, to_apply=%region_35.36 | reduce | flops 414720 | bytes 1880068 | tf_op jit(solution)/shard_map/reduce_sum | solution.py:263
  158.0 0.7 broadcast_multiply_fusion
  (190 shorter events, 2.0 us)
Async XLA Ops:
  7.2 23.3 %all-gather.7.cloned.1.call-start = ((), (), s32[]{:S(2)}) async-start(), calls=%async_computation.6 | async-start | bytes 2359296 | tf_op jit(solution)/shard_map/all_gather | solution.py:134
  9.6 24.4 %all-gather.11.cloned.1.call-start = ((), (), s32[]{:S(2)}) async-start(), calls=%async_computation.8 | async-start | bytes 1572864 | tf_op jit(solution)/shard_map/all_gather | solution.py:133
  10.4 38.5 %all-gather.9.cloned.1.call-start = ((), (), s32[]{:S(2)}) async-start(), calls=%async_computation.7 | async-start | bytes 4718592 | tf_op jit(solution)/shard_map/all_gather | solution.py:132
  11.1 10.5 %collective-permute-start = (bf16[1,1,8,16,1024]{4,3,2,1,0:T(8,128)(2,1)S(1)}, bf16[1,1,8,16,1024]{4,3,2,1,0:T(8,128)(2,1)S(1)}, u32[]{:S(2)}, u32[]{:S(2)}) collective-permute-start(bf16[1,1,8,16,1024]{4,3,2,1,0:T(8,128)(2,1)S(1)} %copy-done.5), channel_id=1, source_target_pairs={{0,4},{4,8},{8,12},{1,5},{5,9},{9,13},{2,6},{6,10},{10,14},{3,7},{... | collective-permute-start | bytes 786440 | tf_op jit(solution)/shard_map/ppermute | solution.py:18
  16.0 9.7 %collective-permute-start.1 = (bf16[1,1,8,16,1024]{4,3,2,1,0:T(8,128)(2,1)S(1)}, bf16[1,1,8,16,1024]{4,3,2,1,0:T(8,128)(2,1)S(1)}, u32[]{:S(2)}, u32[]{:S(2)}) collective-permute-start(bf16[1,1,8,16,1024]{4,3,2,1,0:T(8,128)(2,1)S(1)} %copy-done.5), channel_id=1, source_target_pairs={{4,0},{8,4},{12,8},{5,1},{9,5},{13,9},{6,2},{10,6},{14,10},{7,3},{... | collective-permute-start | bytes 786440 | tf_op jit(solution)/shard_map/ppermute | solution.py:19
  18.1 11.6 %copy-start.20 = (f32[1,1024]{1,0:T(1,128)}, f32[1,1024]{1,0:T(1,128)S(1)}, u32[]{:S(2)}) copy-start(f32[1,1024]{1,0:T(1,128)S(1)} %get-tuple-element.85) | copy-start | bytes 12292
  18.1 11.6 %copy-start.22 = (f32[1,1024]{1,0:T(1,128)}, f32[1,1024]{1,0:T(1,128)S(1)}, u32[]{:S(2)}) copy-start(f32[1,1024]{1,0:T(1,128)S(1)} %get-tuple-element.86) | copy-start | bytes 12292
  18.1 11.6 %copy-start.24 = (f32[1,1024]{1,0:T(1,128)}, f32[1,1024]{1,0:T(1,128)S(1)}, u32[]{:S(2)}) copy-start(f32[1,1024]{1,0:T(1,128)S(1)} %get-tuple-element.87) | copy-start | bytes 12292
  18.1 11.6 %copy-start.26 = (f32[1,1024]{1,0:T(1,128)}, f32[1,1024]{1,0:T(1,128)S(1)}, u32[]{:S(2)}) copy-start(f32[1,1024]{1,0:T(1,128)S(1)} %get-tuple-element.88) | copy-start | bytes 12292
  18.2 11.6 %copy-start.28 = (f32[1,1024]{1,0:T(1,128)}, f32[1,1024]{1,0:T(1,128)S(1)}, u32[]{:S(2)}) copy-start(f32[1,1024]{1,0:T(1,128)S(1)} %get-tuple-element.89) | copy-start | bytes 12292
  18.2 11.6 %copy-start.30 = (f32[1,1024]{1,0:T(1,128)}, f32[1,1024]{1,0:T(1,128)S(1)}, u32[]{:S(2)}) copy-start(f32[1,1024]{1,0:T(1,128)S(1)} %get-tuple-element.90) | copy-start | bytes 12292
  18.3 11.5 %copy-start.32 = (f32[1,1024]{1,0:T(1,128)}, f32[1,1024]{1,0:T(1,128)S(1)}, u32[]{:S(2)}) copy-start(f32[1,1024]{1,0:T(1,128)S(1)} %get-tuple-element.64) | copy-start | bytes 12292
  18.3 11.5 %copy-start.34 = (f32[1,1024]{1,0:T(1,128)}, f32[1,1024]{1,0:T(1,128)S(1)}, u32[]{:S(2)}) copy-start(f32[1,1024]{1,0:T(1,128)S(1)} %get-tuple-element.65) | copy-start | bytes 12292
  18.3 11.5 %copy-start.36 = (f32[1,1024]{1,0:T(1,128)}, f32[1,1024]{1,0:T(1,128)S(1)}, u32[]{:S(2)}) copy-start(f32[1,1024]{1,0:T(1,128)S(1)} %get-tuple-element.66) | copy-start | bytes 12292
  18.3 11.5 %copy-start.38 = (f32[1,1024]{1,0:T(1,128)}, f32[1,1024]{1,0:T(1,128)S(1)}, u32[]{:S(2)}) copy-start(f32[1,1024]{1,0:T(1,128)S(1)} %get-tuple-element.67) | copy-start | bytes 12292
  18.3 11.5 %copy-start.40 = (f32[1,1024]{1,0:T(1,128)}, f32[1,1024]{1,0:T(1,128)S(1)}, u32[]{:S(2)}) copy-start(f32[1,1024]{1,0:T(1,128)S(1)} %get-tuple-element.68) | copy-start | bytes 12292
  18.3 11.5 %copy-start.42 = (f32[1,1024]{1,0:T(1,128)}, f32[1,1024]{1,0:T(1,128)S(1)}, u32[]{:S(2)}) copy-start(f32[1,1024]{1,0:T(1,128)S(1)} %get-tuple-element.69) | copy-start | bytes 12292
  18.3 11.5 %copy-start.44 = (f32[1,1024]{1,0:T(1,128)}, f32[1,1024]{1,0:T(1,128)S(1)}, u32[]{:S(2)}) copy-start(f32[1,1024]{1,0:T(1,128)S(1)} %get-tuple-element.70) | copy-start | bytes 12292
  18.3 11.5 %copy-start.46 = (f32[1,1024]{1,0:T(1,128)}, f32[1,1024]{1,0:T(1,128)S(1)}, u32[]{:S(2)}) copy-start(f32[1,1024]{1,0:T(1,128)S(1)} %get-tuple-element.71) | copy-start | bytes 12292
  18.3 11.5 %copy-start.48 = (f32[1,1024]{1,0:T(1,128)}, f32[1,1024]{1,0:T(1,128)S(1)}, u32[]{:S(2)}) copy-start(f32[1,1024]{1,0:T(1,128)S(1)} %get-tuple-element.72) | copy-start | bytes 12292
  18.4 11.5 %copy-start.50 = (f32[1,1024]{1,0:T(1,128)}, f32[1,1024]{1,0:T(1,128)S(1)}, u32[]{:S(2)}) copy-start(f32[1,1024]{1,0:T(1,128)S(1)} %get-tuple-element.73) | copy-start | bytes 12292
  18.4 11.5 %copy-start.52 = (f32[1,1024]{1,0:T(1,128)}, f32[1,1024]{1,0:T(1,128)S(1)}, u32[]{:S(2)}) copy-start(f32[1,1024]{1,0:T(1,128)S(1)} %get-tuple-element.74) | copy-start | bytes 12292
  18.4 11.5 %copy-start.54 = (f32[1,1024]{1,0:T(1,128)}, f32[1,1024]{1,0:T(1,128)S(1)}, u32[]{:S(2)}) copy-start(f32[1,1024]{1,0:T(1,128)S(1)} %get-tuple-element.75) | copy-start | bytes 12292
  29.5 12.8 %copy-start.14 = (f32[8,16]{1,0:T(8,128)}, f32[8,16]{1,0:T(8,128)S(1)}, u32[]{:S(2)}) copy-start(f32[8,16]{1,0:T(8,128)S(1)} %broadcast_multiply_fusion.1) | copy-start | bytes 1540
  32.6 16.2 %copy-start.70 = (f32[1,1,1024]{2,0,1:T(1,128)}, f32[1,1,1024]{2,0,1:T(1,128)S(1)}, u32[]{:S(2)}) copy-start(f32[1,1,1024]{2,0,1:T(1,128)S(1)} %get-tuple-element.91) | copy-start | bytes 12292
  32.6 16.2 %copy-start.72 = (f32[1,1,1024]{2,0,1:T(1,128)}, f32[1,1,1024]{2,0,1:T(1,128)S(1)}, u32[]{:S(2)}) copy-start(f32[1,1,1024]{2,0,1:T(1,128)S(1)} %get-tuple-element.93) | copy-start | bytes 12292
  36.4 19.2 %all-to-all-start.3 = ((bf16[4,128,128]{1,2,0:T(8,128)(2,1)}), bf16[4,128,128]{1,2,0:T(8,128)(2,1)S(1)}, u32[]{:S(2)}, u32[]{:S(2)}) async-start(bf16[4,128,128]{1,2,0:T(8,128)(2,1)} %bitcast.65), calls=%async_computation.3 | async-start | bytes 262144 | tf_op jit(solution)/shard_map/all_to_all | solution.py:179
  55.6 11.2 %all-to-all-start.1 = ((bf16[4,128,128]{1,2,0:T(8,128)(2,1)}), bf16[4,128,128]{1,2,0:T(8,128)(2,1)S(1)}, u32[]{:S(2)}, u32[]{:S(2)}) async-start(bf16[4,128,128]{1,2,0:T(8,128)(2,1)} %bitcast.54), calls=%async_computation.1 | async-start | bytes 262144 | tf_op jit(solution)/shard_map/all_to_all | solution.py:176
  66.8 11.6 %all-to-all-start = ((bf16[4,128,256]{1,2,0:T(8,128)(2,1)}), bf16[4,128,256]{1,2,0:T(8,128)(2,1)S(1)}, u32[]{:S(2)}, u32[]{:S(2)}) async-start(bf16[4,128,256]{1,2,0:T(8,128)(2,1)} %bitcast.50), calls=%async_computation | async-start | bytes 524288 | tf_op jit(solution)/shard_map/all_to_all | solution.py:195
  82.3 10.2 %all-to-all-start.4 = ((bf16[4,128,256]{1,2,0:T(8,128)(2,1)}), bf16[4,128,256]{1,2,0:T(8,128)(2,1)S(1)}, u32[]{:S(2)}, u32[]{:S(2)}) async-start(bf16[4,128,256]{1,2,0:T(8,128)(2,1)} %copy.48), calls=%async_computation.4 | async-start | bytes 524288 | tf_op jit(solution)/shard_map/all_to_all | solution.py:227
  92.5 10.9 %all-to-all-start.5 = ((f32[4,128,128]{1,2,0:T(8,128)}), f32[4,128,128]{1,2,0:T(8,128)}, u32[]{:S(2)}, u32[]{:S(2)}) async-start(f32[4,128,128]{1,2,0:T(8,128)} %copy.50), calls=%async_computation.5 | async-start | bytes 524288 | tf_op jit(solution)/shard_map/all_to_all | solution.py:218
  96.5 59.7 %all-gather.13.cloned.1.call-start = ((), (), s32[]{:S(2)}) async-start(), calls=%async_computation.9 | async-start | bytes 2228224 | tf_op jit(solution)/shard_map/all_gather | solution.py:263
  108.7 16.0 %copy-start.4 = (bf16[512,1024]{1,0:T(8,128)(2,1)S(1)}, bf16[512,1024]{1,0:T(8,128)(2,1)}, u32[]{:S(2)}) copy-start(bf16[512,1024]{1,0:T(8,128)(2,1)} %all-gather.11.cloned.1.call-done) | copy-start | bytes 3145732
  108.7 16.0 %copy-start.71 = (f32[1,1,1024]{2,0,1:T(1,128)S(1)}, f32[1,1,1024]{2,0,1:T(1,128)}, u32[]{:S(2)}) copy-start(f32[1,1,1024]{2,0,1:T(1,128)} %copy-done.70) | copy-start | bytes 12292
  114.3 15.7 %copy-start.17 = (f32[1,1024]{1,0:T(1,128)S(1)}, f32[1,1024]{1,0:T(1,128)}, u32[]{:S(2)}) copy-start(f32[1,1024]{1,0:T(1,128)} %copy-done.16) | copy-start | bytes 12292
  114.3 15.7 %copy-start.19 = (f32[1,1024]{1,0:T(1,128)S(1)}, f32[1,1024]{1,0:T(1,128)}, u32[]{:S(2)}) copy-start(f32[1,1024]{1,0:T(1,128)} %copy-done.18) | copy-start | bytes 12292
  114.3 15.7 %copy-start.21 = (f32[1,1024]{1,0:T(1,128)S(1)}, f32[1,1024]{1,0:T(1,128)}, u32[]{:S(2)}) copy-start(f32[1,1024]{1,0:T(1,128)} %copy-done.20) | copy-start | bytes 12292
  114.3 15.7 %copy-start.23 = (f32[1,1024]{1,0:T(1,128)S(1)}, f32[1,1024]{1,0:T(1,128)}, u32[]{:S(2)}) copy-start(f32[1,1024]{1,0:T(1,128)} %copy-done.22) | copy-start | bytes 12292
  114.3 15.7 %copy-start.25 = (f32[1,1024]{1,0:T(1,128)S(1)}, f32[1,1024]{1,0:T(1,128)}, u32[]{:S(2)}) copy-start(f32[1,1024]{1,0:T(1,128)} %copy-done.24) | copy-start | bytes 12292
  114.3 15.7 %copy-start.27 = (f32[1,1024]{1,0:T(1,128)S(1)}, f32[1,1024]{1,0:T(1,128)}, u32[]{:S(2)}) copy-start(f32[1,1024]{1,0:T(1,128)} %copy-done.26) | copy-start | bytes 12292
  114.3 15.7 %copy-start.29 = (f32[1,1024]{1,0:T(1,128)S(1)}, f32[1,1024]{1,0:T(1,128)}, u32[]{:S(2)}) copy-start(f32[1,1024]{1,0:T(1,128)} %copy-done.28) | copy-start | bytes 12292
  114.3 15.7 %copy-start.31 = (f32[1,1024]{1,0:T(1,128)S(1)}, f32[1,1024]{1,0:T(1,128)}, u32[]{:S(2)}) copy-start(f32[1,1024]{1,0:T(1,128)} %copy-done.30) | copy-start | bytes 12292
  114.3 15.7 %copy-start.33 = (f32[1,1024]{1,0:T(1,128)S(1)}, f32[1,1024]{1,0:T(1,128)}, u32[]{:S(2)}) copy-start(f32[1,1024]{1,0:T(1,128)} %copy-done.32) | copy-start | bytes 12292
  114.3 15.7 %copy-start.35 = (f32[1,1024]{1,0:T(1,128)S(1)}, f32[1,1024]{1,0:T(1,128)}, u32[]{:S(2)}) copy-start(f32[1,1024]{1,0:T(1,128)} %copy-done.34) | copy-start | bytes 12292
  114.3 15.7 %copy-start.37 = (f32[1,1024]{1,0:T(1,128)S(1)}, f32[1,1024]{1,0:T(1,128)}, u32[]{:S(2)}) copy-start(f32[1,1024]{1,0:T(1,128)} %copy-done.36) | copy-start | bytes 12292
  114.3 15.7 %copy-start.39 = (f32[1,1024]{1,0:T(1,128)S(1)}, f32[1,1024]{1,0:T(1,128)}, u32[]{:S(2)}) copy-start(f32[1,1024]{1,0:T(1,128)} %copy-done.38) | copy-start | bytes 12292
  114.3 15.7 %copy-start.41 = (f32[1,1024]{1,0:T(1,128)S(1)}, f32[1,1024]{1,0:T(1,128)}, u32[]{:S(2)}) copy-start(f32[1,1024]{1,0:T(1,128)} %copy-done.40) | copy-start | bytes 12292
  114.4 15.7 %copy-start.43 = (f32[1,1024]{1,0:T(1,128)S(1)}, f32[1,1024]{1,0:T(1,128)}, u32[]{:S(2)}) copy-start(f32[1,1024]{1,0:T(1,128)} %copy-done.42) | copy-start | bytes 12292
  114.4 15.7 %copy-start.45 = (f32[1,1024]{1,0:T(1,128)S(1)}, f32[1,1024]{1,0:T(1,128)}, u32[]{:S(2)}) copy-start(f32[1,1024]{1,0:T(1,128)} %copy-done.44) | copy-start | bytes 12292
  114.4 15.7 %copy-start.47 = (f32[1,1024]{1,0:T(1,128)S(1)}, f32[1,1024]{1,0:T(1,128)}, u32[]{:S(2)}) copy-start(f32[1,1024]{1,0:T(1,128)} %copy-done.46) | copy-start | bytes 12292
  114.4 15.7 %copy-start.49 = (f32[1,1024]{1,0:T(1,128)S(1)}, f32[1,1024]{1,0:T(1,128)}, u32[]{:S(2)}) copy-start(f32[1,1024]{1,0:T(1,128)} %copy-done.48) | copy-start | bytes 12292
  114.4 15.7 %copy-start.51 = (f32[1,1024]{1,0:T(1,128)S(1)}, f32[1,1024]{1,0:T(1,128)}, u32[]{:S(2)}) copy-start(f32[1,1024]{1,0:T(1,128)} %copy-done.50) | copy-start | bytes 12292
  114.4 15.7 %copy-start.53 = (f32[1,1024]{1,0:T(1,128)S(1)}, f32[1,1024]{1,0:T(1,128)}, u32[]{:S(2)}) copy-start(f32[1,1024]{1,0:T(1,128)} %copy-done.52) | copy-start | bytes 12292
  114.4 15.7 %copy-start.55 = (f32[1,1024]{1,0:T(1,128)S(1)}, f32[1,1024]{1,0:T(1,128)}, u32[]{:S(2)}) copy-start(f32[1,1024]{1,0:T(1,128)} %copy-done.54) | copy-start | bytes 12292
  114.4 15.7 %copy-start.57 = (f32[1,1024]{1,0:T(1,128)S(1)}, f32[1,1024]{1,0:T(1,128)}, u32[]{:S(2)}) copy-start(f32[1,1024]{1,0:T(1,128)} %copy-done.56) | copy-start | bytes 12292
  114.4 15.7 %copy-start.59 = (f32[1,1024]{1,0:T(1,128)S(1)}, f32[1,1024]{1,0:T(1,128)}, u32[]{:S(2)}) copy-start(f32[1,1024]{1,0:T(1,128)} %copy-done.58) | copy-start | bytes 12292
  114.4 15.7 %copy-start.61 = (f32[1,1024]{1,0:T(1,128)S(1)}, f32[1,1024]{1,0:T(1,128)}, u32[]{:S(2)}) copy-start(f32[1,1024]{1,0:T(1,128)} %copy-done.60) | copy-start | bytes 12292
  114.5 15.7 %copy-start.63 = (f32[1,1024]{1,0:T(1,128)S(1)}, f32[1,1024]{1,0:T(1,128)}, u32[]{:S(2)}) copy-start(f32[1,1024]{1,0:T(1,128)} %copy-done.62) | copy-start | bytes 12292
  114.5 15.7 %copy-start.65 = (f32[1,1024]{1,0:T(1,128)S(1)}, f32[1,1024]{1,0:T(1,128)}, u32[]{:S(2)}) copy-start(f32[1,1024]{1,0:T(1,128)} %copy-done.64) | copy-start | bytes 12292
  114.5 15.7 %copy-start.67 = (f32[1,1024]{1,0:T(1,128)S(1)}, f32[1,1024]{1,0:T(1,128)}, u32[]{:S(2)}) copy-start(f32[1,1024]{1,0:T(1,128)} %copy-done.66) | copy-start | bytes 12292
  114.5 15.7 %copy-start.69 = (f32[1,1024]{1,0:T(1,128)S(1)}, f32[1,1024]{1,0:T(1,128)}, u32[]{:S(2)}) copy-start(f32[1,1024]{1,0:T(1,128)} %copy-done.68) | copy-start | bytes 12292
  115.2 9.4 %all-to-all-start.2 = ((bf16[4,128,128]{1,2,0:T(8,128)(2,1)}), bf16[4,128,128]{1,2,0:T(8,128)(2,1)S(1)}, u32[]{:S(2)}, u32[]{:S(2)}) async-start(bf16[4,128,128]{1,2,0:T(8,128)(2,1)} %copy.42), calls=%async_computation.2 | async-start | bytes 262144 | tf_op jit(solution)/shard_map/all_to_all | solution.py:207
  118.7 10.0 %collective-permute-start.3 = (bf16[1,1,8,16,1024]{4,3,2,1,0:T(8,128)(2,1)S(1)}, bf16[1,1,8,16,1024]{4,3,2,1,0:T(8,128)(2,1)S(1)}, u32[]{:S(2)}, u32[]{:S(2)}) collective-permute-start(bf16[1,1,8,16,1024]{4,3,2,1,0:T(8,128)(2,1)S(1)} %bitcast.245), channel_id=1, source_target_pairs={{4,0},{8,4},{12,8},{5,1},{9,5},{13,9},{6,2},{10,6},{14,10},{7,3},{... | collective-permute-start | bytes 786440 | tf_op jit(solution)/shard_map/ppermute | solution.py:19
  119.9 9.9 %collective-permute-start.2 = (bf16[1,1,8,16,1024]{4,3,2,1,0:T(8,128)(2,1)S(1)}, bf16[1,1,8,16,1024]{4,3,2,1,0:T(8,128)(2,1)S(1)}, u32[]{:S(2)}, u32[]{:S(2)}) collective-permute-start(bf16[1,1,8,16,1024]{4,3,2,1,0:T(8,128)(2,1)S(1)} %bitcast.246), channel_id=1, source_target_pairs={{0,4},{4,8},{8,12},{1,5},{5,9},{9,13},{2,6},{6,10},{10,14},{3,7},{... | collective-permute-start | bytes 786440 | tf_op jit(solution)/shard_map/ppermute | solution.py:18
  (28 other events, 182.2 us)
Sparse Core Ops, SparseCore 0:
  9.7 12.3 all-gather.6
  23.7 10.2 all-gather.10
  35.5 13.2 all-gather.8
  114.6 41.5 all-gather.12
